TPU v7x, 32 devices: a whole 2x2x4 slice. The times are simulated.
32 devices in a mesh: section: 4 (over y, x), tp: 8 (over z, core).
Axes of the slice: x: 2, y: 2, z: 4, core: 2. Of those that a mesh axis runs over, the one named last changes fastest.
Arguments:
- inputs_now: bfloat16 [1536, 6144], P(('section', 'tp')), may hold values from -6 to 6
- cotangents: bfloat16 [1536, 6144], P(('section', 'tp')), may hold values from -6 to 6
- stashed: bfloat16 [3, 1536, 6144], P(None, ('section', 'tp')), may hold values from -6 to 6
- plan: int32 [4], replicated, may hold values from 0 to 2
- fwd_scores: bfloat16 [4, 48, 384, 384], P('section', 'tp'), may hold values from -9 to 300, as said below
- back_scores: bfloat16 [4, 48, 384, 384], P('section', 'tp'), may hold values from -9 to 300, as said below
- value_weight: bfloat16 [4, 6144, 6144], P('section', None, 'tp'), may hold values from -0.078125 to 0.078125
- out_weight: bfloat16 [4, 6144, 6144], P('section', 'tp'), may hold values from -0.21875 to 0.21875
Outputs:
- handed_on: bfloat16 [1536, 6144], P(('section', 'tp'))
- grad_back: bfloat16 [1536, 6144], P(('section', 'tp'))
- stash_next: bfloat16 [3, 1536, 6144], P(None, ('section', 'tp'))
- value_grad: bfloat16 [4, 6144, 6144], P('section', None, 'tp')
- out_grad: bfloat16 [4, 6144, 6144], P('section', 'tp')
Inputs may be any that keep to these rules, and one draw needn't show every extreme that they name: plan[s] names the slot, in the stash rows of section 3 - s, that holds section s's micro-batch for this tick's backward. `fwd_scores`: logits of keys later than the query are never read. `back_scores`: logits of keys later than the query are never read.
All inputs are finite; a program needn't handle non-finite values.
Results may differ from a plain program's by a relative error of at most 0.012.
Values may be sent and summed in bfloat16 or wider, within the bound.
A program may use at most 192 MiB of HBM per device.

v0:
```python
import jax
import jax.numpy as jnp
from jax import lax
from jax.sharding import PartitionSpec as P

HEAD = 128
eps = 1e-05


def passed_along(array, axis, by):
    size = lax.axis_size(axis)
    return lax.ppermute(array, axis, [(i, (i + by) % size) for i in range(size)])


def partner(value, axis, stride):
    mask = 2**stride
    pairs = [(source, source ^ mask) for source in range(lax.axis_size(axis))]
    return lax.ppermute(value, axis, pairs)


def normalize(layer_rows):
    average = jnp.mean(layer_rows, axis=-1, keepdims=True)
    centred = layer_rows - average
    inv_scale = lax.rsqrt(jnp.mean(centred * centred, axis=-1, keepdims=True) + eps)
    return (centred * inv_scale, inv_scale)


def causal_softmax(scores):
    logits = scores.astype(jnp.float32)
    rows = logits.shape[-1]
    causal = lax.broadcasted_iota(jnp.int32, (rows, rows), 0) >= lax.broadcasted_iota(
        jnp.int32, (rows, rows), 1
    )
    logits = jnp.where(causal, logits, -1e30)
    row_top = jnp.max(logits, axis=-1, keepdims=True)
    raised = jnp.where(causal, jnp.exp(logits - row_top), 0.0)
    return (raised / jnp.sum(raised, axis=-1, keepdims=True)).astype(jnp.bfloat16)


def mix_heads(weights, value_rows):
    rows = value_rows.shape[0]
    head_count = weights.shape[0]
    by_head = value_rows.reshape(rows, head_count, HEAD)
    mixed = jnp.einsum("hqk,khe->qhe", weights, by_head, preferred_element_type=jnp.float32)
    return mixed.reshape(rows, head_count * HEAD).astype(jnp.bfloat16)


def per_device(
    inputs_now, cotangents, stashed, plan, fwd_scores, back_scores, value_weight, out_weight
):
    tp_count = lax.axis_size("tp")
    sections = lax.axis_size("section")
    tp_index = lax.axis_index("tp")
    section_idx = lax.axis_index("section")
    mirror = sections - 1 - section_idx
    share_rows = inputs_now.shape[0]
    all_rows = share_rows * tp_count
    weight_in = value_weight[0]
    weight_out = out_weight[0]
    col_share = weight_in.shape[1]
    layer_rows = inputs_now.astype(jnp.float32)
    unit_rows, _ = normalize(layer_rows)
    normed = unit_rows.astype(jnp.bfloat16)
    values = jnp.dot(
        lax.all_gather(normed, "tp", axis=0, tiled=True),
        weight_in,
        preferred_element_type=jnp.float32,
    ).astype(jnp.bfloat16)
    context = mix_heads(causal_softmax(fwd_scores[0]), values)
    summed = lax.psum(
        jnp.dot(context, weight_out, preferred_element_type=jnp.float32).astype(jnp.bfloat16), "tp"
    ).astype(jnp.float32)
    branch = lax.dynamic_slice_in_dim(summed, tp_index * share_rows, share_rows, 0)
    layer_out = (layer_rows + branch).astype(jnp.bfloat16)
    handed_on = passed_along(layer_out, "section", 1)
    lookup = jnp.arange(sections, dtype=jnp.int32)
    owner_slot = jnp.sum(jnp.where(lookup == mirror, plan, 0))
    guest_rows = lax.dynamic_index_in_dim(stashed, owner_slot, 0, keepdims=False)
    outgoing = jnp.stack([guest_rows, inputs_now])
    incoming = outgoing
    for flip_bit in range(sections.bit_length() - 1):
        incoming = partner(incoming, "section", flip_bit)
    stored = incoming[0]
    arrived = incoming[1]
    stash_next = lax.dynamic_update_index_in_dim(stashed, arrived, owner_slot, 0)
    stash_unit, stash_scale = normalize(stored.astype(jnp.float32))
    stash_normed = stash_unit.astype(jnp.bfloat16)
    piece_norm = lax.all_gather(stash_normed, "tp", axis=0, tiled=True)
    piece_cot = lax.all_gather(cotangents, "tp", axis=0, tiled=True)
    rows_norm = piece_norm
    rows_cot = piece_cot
    piece_value = jnp.dot(piece_norm, weight_in, preferred_element_type=jnp.float32).astype(
        jnp.bfloat16
    )
    rows_value = piece_value
    piece_grad = jnp.einsum(
        "td,hd->th", piece_cot, weight_out, preferred_element_type=jnp.float32
    ).astype(jnp.bfloat16)
    rows_grad = piece_grad
    rows_norm, rows_cot, rows_value, rows_grad = (rows_norm, rows_cot, rows_value, rows_grad)
    back_probs = causal_softmax(back_scores[0])
    stash_context = mix_heads(back_probs, rows_value)
    grad_outw = jnp.einsum("th,td->hd", stash_context, rows_cot, preferred_element_type=jnp.float32)
    head_count = back_probs.shape[0]
    value_back = (
        jnp.einsum(
            "hqk,qhe->khe",
            back_probs,
            rows_grad.reshape(all_rows, head_count, HEAD),
            preferred_element_type=jnp.float32,
        )
        .reshape(all_rows, col_share)
        .astype(jnp.bfloat16)
    )
    grad_valw = jnp.einsum("td,th->dh", rows_norm, value_back, preferred_element_type=jnp.float32)
    summed_back = lax.psum(
        jnp.einsum("th,dh->td", value_back, weight_in, preferred_element_type=jnp.float32).astype(
            jnp.bfloat16
        ),
        "tp",
    ).astype(jnp.float32)
    norm_grad = lax.dynamic_slice_in_dim(summed_back, tp_index * share_rows, share_rows, 0)
    input_grad = cotangents.astype(jnp.float32) + stash_scale * (
        norm_grad
        - jnp.mean(norm_grad, axis=-1, keepdims=True)
        - stash_unit * jnp.mean(norm_grad * stash_unit, axis=-1, keepdims=True)
    )
    grad_back = passed_along(input_grad.astype(jnp.bfloat16), "section", -1)
    return (
        handed_on,
        grad_back,
        stash_next,
        grad_valw.astype(jnp.bfloat16)[None],
        grad_outw.astype(jnp.bfloat16)[None],
    )


def solution(mesh):
    return jax.shard_map(
        per_device,
        mesh=mesh,
        in_specs=(
            P(("section", "tp"), None),
            P(("section", "tp"), None),
            P(None, ("section", "tp"), None),
            P(),
            P("section", "tp", None, None),
            P("section", "tp", None, None),
            P("section", None, "tp"),
            P("section", "tp", None),
        ),
        out_specs=(
            P(("section", "tp"), None),
            P(("section", "tp"), None),
            P(None, ("section", "tp"), None),
            P("section", None, "tp"),
            P("section", "tp", None),
        ),
        check_vma=False,
    )
```

profile of v0, /device:TPU:0, one launch (start us, length us, event | category | flops | bytes accessed | tf_op | source)
XLA Modules:
  0.0 429.3 jit_solution(4196626282191384859)
XLA Ops:
  7.2 2.9 copy.25
  12.6 5.9 %fusion.64 = (f32[6,384]{1,0:T(8,128)S(1)}, f32[6,384,384]{2,1,0:T(8,128)}) fusion(bf16[1,6,384,384]{3,2,1,0:T(8,128)(2,1)} %param.12, pred[384,384]{1,0:T(8,128)(4,1)S(1)} %iota_compare_fusion), kind=kOutput, calls=%fused_computation.81 | output fusion | flops 6193535 | bytes 5465088 | tf_op jit(solution)/shard_map/sub | solution.py:36
  18.5 2.2 fusion.65
  21.1 44.7 %all-gather.4.cloned.1.call-done = bf16[384,6144]{1,0:T(8,128)(2,1)} async-done(((bf16[48,6144]{1,0:T(8,128)(2,1)}), bf16[384,6144]{1,0:T(8,128)(2,1)}) %all-gather.4.cloned.1.call-update) | async-done | bytes 4718608 | tf_op jit(solution)/shard_map/all_gather | solution.py:65
  65.8 8.9 %fusion.38 = bf16[384,768]{1,0:T(8,128)(2,1)S(1)} fusion(bf16[384,6144]{1,0:T(8,128)(2,1)} %all-gather.4.cloned.1.call-done, bf16[1,6144,768]{2,1,0:T(8,128)(2,1)} %param.14), kind=kOutput, calls=%fused_computation.48 | convolution fusion | flops 3624173568 | bytes 14745600 | tf_op jit(solution)/shard_map/dot_general | solution.py:64
  75.0 2.8 fusion.37
  77.8 9.5 %fusion.17 = bf16[384,6144]{1,0:T(8,128)(2,1)} fusion(bf16[384,768]{0,1:T(8,128)(2,1)S(1)} %bitcast.100, bf16[1,768,6144]{2,1,0:T(8,128)(2,1)} %param.15), kind=kOutput, calls=%fused_computation.17 | convolution fusion | flops 3626237952 | bytes 14745600 | tf_op jit(solution)/shard_map/dot_general | solution.py:71
  87.3 30.2 %all-gather.6.cloned.1.call-done = bf16[384,6144]{1,0:T(8,128)(2,1)} async-done(((bf16[48,6144]{1,0:T(8,128)(2,1)}), bf16[384,6144]{1,0:T(8,128)(2,1)}) %all-gather.6.cloned.1.call-update) | async-done | bytes 4718608 | tf_op jit(solution)/shard_map/all_gather | solution.py:89
  117.4 9.0 %fusion.44 = bf16[384,768]{1,0:T(8,128)(2,1)S(1)} fusion(bf16[384,6144]{1,0:T(8,128)(2,1)} %all-gather.6.cloned.1.call-done, bf16[1,768,6144]{2,1,0:T(8,128)(2,1)} %param.15), kind=kOutput, calls=%fused_computation.50 | convolution fusion | flops 3624173568 | bytes 14745600 | tf_op jit(solution)/shard_map/td,hd->th/dot_general | solution.py:96
  128.1 14.5 %fusion.14 = bf16[384,6144]{1,0:T(8,128)(2,1)} fusion(bf16[384,768]{0,1:T(8,128)(2,1)S(1)} %bitcast.102, bf16[1,6144,768]{2,1,0:T(8,128)(2,1)} %param.14), kind=kOutput, calls=%fused_computation.16 | convolution fusion | flops 3626237952 | bytes 14745600 | tf_op jit(solution)/shard_map/th,dh->td/dot_general | solution.py:117
  148.6 26.8 %collective-permute-done.1 = bf16[2,48,6144]{2,1,0:T(8,128)(2,1)} collective-permute-done((bf16[2,48,6144]{2,1,0:T(8,128)(2,1)S(1)}, bf16[2,48,6144]{2,1,0:T(8,128)(2,1)}, u32[]{:S(2)}, u32[]{:S(2)}) %collective-permute-start.1) | collective-permute-done | bytes 1179680 | tf_op jit(solution)/shard_map/ppermute | solution.py:18
  176.8 26.0 %collective-permute-done.2 = bf16[2,48,6144]{2,1,0:T(8,128)(2,1)S(1)} collective-permute-done((bf16[2,48,6144]{2,1,0:T(8,128)(2,1)}, bf16[2,48,6144]{2,1,0:T(8,128)(2,1)S(1)}, u32[]{:S(2)}, u32[]{:S(2)}) %collective-permute-start.2) | collective-permute-done | bytes 1179680 | tf_op jit(solution)/shard_map/ppermute | solution.py:18
  203.4 133.5 %all-reduce.3.cloned.1.call-done = (bf16[384,6144]{1,0:T(8,128)(2,1)}, bf16[384,6144]{1,0:T(8,128)(2,1)}) async-done(((bf16[384,6144]{1,0:T(8,128)(2,1)}, bf16[384,6144]{1,0:T(8,128)(2,1)}), (bf16[384,6144]{1,0:T(8,128)(2,1)}, bf16[384,6144]{1,0:T(8,128)(2,1)})) %all-reduce.3.cloned.1.call-update) | async-done | bytes 9437200 | tf_op jit(solution)/shard_map/psum | solution.py:70
  336.9 1.5 convert_reduce_fusion
  338.4 2.7 fusion.52
  342.3 1.5 collective-permute-start
  343.9 1.5 collective-permute-start.3
  346.2 13.3 %collective-permute-done = bf16[48,6144]{1,0:T(8,128)(2,1)S(1)} collective-permute-done((bf16[48,6144]{1,0:T(8,128)(2,1)S(1)}, bf16[48,6144]{1,0:T(8,128)(2,1)S(1)}, u32[]{:S(2)}, u32[]{:S(2)}) %collective-permute-start) | collective-permute-done | bytes 589856 | tf_op jit(solution)/shard_map/ppermute | solution.py:12
  359.5 11.3 %collective-permute-done.3 = bf16[48,6144]{1,0:T(8,128)(2,1)} collective-permute-done((bf16[48,6144]{1,0:T(8,128)(2,1)}, bf16[48,6144]{1,0:T(8,128)(2,1)}, u32[]{:S(2)}, u32[]{:S(2)}) %collective-permute-start.3) | collective-permute-done | bytes 589856 | tf_op jit(solution)/shard_map/ppermute | solution.py:12
  370.8 21.8 %all-gather.8.cloned.1.call-done = bf16[384,6144]{1,0:T(8,128)(2,1)} async-done(((bf16[48,6144]{1,0:T(8,128)(2,1)}), bf16[384,6144]{1,0:T(8,128)(2,1)}) %all-gather.8.cloned.1.call-update) | async-done | bytes 4718608 | tf_op jit(solution)/shard_map/all_gather | solution.py:88
  392.6 8.9 %fusion.41 = bf16[384,768]{1,0:T(8,128)(2,1)S(1)} fusion(bf16[384,6144]{1,0:T(8,128)(2,1)} %all-gather.8.cloned.1.call-done, bf16[1,6144,768]{2,1,0:T(8,128)(2,1)} %param.14), kind=kOutput, calls=%fused_computation.49 | convolution fusion | flops 3624173568 | bytes 14745600 | tf_op jit(solution)/shard_map/dot_general | solution.py:92
  402.6 9.9 %fusion.12 = bf16[1,6144,768]{2,1,0:T(8,128)(2,1)} fusion(bf16[384,6144]{1,0:T(8,128)(2,1)} %all-gather.8.cloned.1.call-done, bf16[384,768]{0,1:T(8,128)(2,1)S(1)} %bitcast.103), kind=kOutput, calls=%fused_computation.14 | convolution fusion | flops 3628597248 | bytes 14745600 | tf_op jit(solution)/shard_map/td,th->dh/dot_general | solution.py:115
  412.5 7.4 %fusion.13 = bf16[1,768,6144]{2,1,0:T(8,128)(2,1)} fusion(bf16[384,768]{0,1:T(8,128)(2,1)S(1)} %bitcast.104, bf16[384,6144]{1,0:T(8,128)(2,1)S(1)} %bitcast.106), kind=kOutput, calls=%fused_computation.15 | convolution fusion | flops 3628597248 | bytes 14745600 | tf_op jit(solution)/shard_map/th,td->hd/dot_general | solution.py:103
  420.8 1.9 copy.27
  (52 shorter events, 14.7 us)
Async XLA Ops:
  7.2 2.9 copy-start
  7.2 58.6 %all-gather.4.cloned.1.call-start = ((), (), s32[]{:S(2)}) async-start(), calls=%async_computation | async-start | bytes 5308416 | tf_op jit(solution)/shard_map/all_gather | solution.py:65
  11.7 105.7 %all-gather.6.cloned.1.call-start = ((), (), s32[]{:S(2)}) async-start(), calls=%async_computation.1 | async-start | bytes 5308416 | tf_op jit(solution)/shard_map/all_gather | solution.py:89
  12.5 324.4 %all-reduce.3.cloned.1.call-start = ((), (), s32[]{:S(2)}) async-start(), calls=%async_computation.3 | async-start | bytes 18874368 | tf_op jit(solution)/shard_map/psum | solution.py:70
  12.6 5.9 %copy-start.5 = (bf16[1,6,384,384]{3,2,1,0:T(8,128)(2,1)S(1)}, bf16[1,6,384,384]{3,2,1,0:T(8,128)(2,1)}, u32[]{:S(2)}) copy-start(bf16[1,6,384,384]{3,2,1,0:T(8,128)(2,1)} %param.13) | copy-start | bytes 5308420
  127.3 0.8 copy-start.3
  142.6 0.7 copy-start.6
  142.6 250.0 %all-gather.8.cloned.1.call-start = ((), (), s32[]{:S(2)}) async-start(), calls=%async_computation.2 | async-start | bytes 5308416 | tf_op jit(solution)/shard_map/all_gather | solution.py:88
  147.1 28.2 %collective-permute-start.1 = (bf16[2,48,6144]{2,1,0:T(8,128)(2,1)S(1)}, bf16[2,48,6144]{2,1,0:T(8,128)(2,1)}, u32[]{:S(2)}, u32[]{:S(2)}) collective-permute-start(bf16[2,48,6144]{2,1,0:T(8,128)(2,1)S(1)} %pad_maximum_fusion), channel_id=1, source_target_pairs={{0,8},{8,0},{16,24},{24,16},{1,9},{9,1},{17,25},{25,17},{2,10},{10... | collective-permute-start | bytes 3538952 | tf_op jit(solution)/shard_map/ppermute | solution.py:18
  175.4 27.4 %collective-permute-start.2 = (bf16[2,48,6144]{2,1,0:T(8,128)(2,1)}, bf16[2,48,6144]{2,1,0:T(8,128)(2,1)S(1)}, u32[]{:S(2)}, u32[]{:S(2)}) collective-permute-start(bf16[2,48,6144]{2,1,0:T(8,128)(2,1)} %collective-permute-done.1), channel_id=1, source_target_pairs={{0,16},{8,24},{16,0},{24,8},{1,17},{9,25},{17,1},{25,9},{2,18},{10... | collective-permute-start | bytes 3538952 | tf_op jit(solution)/shard_map/ppermute | solution.py:18
  342.3 17.2 %collective-permute-start = (bf16[48,6144]{1,0:T(8,128)(2,1)S(1)}, bf16[48,6144]{1,0:T(8,128)(2,1)S(1)}, u32[]{:S(2)}, u32[]{:S(2)}) collective-permute-start(bf16[48,6144]{1,0:T(8,128)(2,1)S(1)} %fusion.59), channel_id=1, source_target_pairs={{0,8},{8,16},{16,24},{24,0},{1,9},{9,17},{17,25},{25,1},{2,10},{10... | collective-permute-start | bytes 1769480 | tf_op jit(solution)/shard_map/ppermute | solution.py:12
  343.9 26.9 %collective-permute-start.3 = (bf16[48,6144]{1,0:T(8,128)(2,1)}, bf16[48,6144]{1,0:T(8,128)(2,1)}, u32[]{:S(2)}, u32[]{:S(2)}) collective-permute-start(bf16[48,6144]{1,0:T(8,128)(2,1)} %get-tuple-element.10), channel_id=1, source_target_pairs={{0,24},{8,0},{16,8},{24,16},{1,25},{9,1},{17,9},{25,17},{2,26},{10... | collective-permute-start | bytes 1769480 | tf_op jit(solution)/shard_map/ppermute | solution.py:12
  359.5 33.1 %copy-start.1 = (bf16[48,6144]{1,0:T(8,128)(2,1)}, bf16[48,6144]{1,0:T(8,128)(2,1)S(1)}, u32[]{:S(2)}) copy-start(bf16[48,6144]{1,0:T(8,128)(2,1)S(1)} %collective-permute-done) | copy-start | bytes 1769476
  401.6 1.1 copy-start.4
  401.9 10.7 %slice-start = ((s8[4718592]{0:T(1024)(128)(4,1)}), s8[4194304]{0:T(1024)(128)(4,1)S(1)}, s32[]{:S(2)}) async-start(s8[4718592]{0:T(1024)(128)(4,1)} %bitcast.105), calls=%async_computation.4 | async-start | bytes 8388608
  402.6 9.9 %slice-start.1 = ((s8[4718592]{0:T(1024)(128)(4,1)}), s8[524288]{0:T(1024)(128)(4,1)S(1)}, s32[]{:S(2)}) async-start(s8[4718592]{0:T(1024)(128)(4,1)} %bitcast.105), calls=%async_computation.5 | async-start | bytes 1048576
  412.5 7.5 %copy-start.2 = (bf16[48,6144]{1,0:T(8,128)(2,1)S(1)}, bf16[48,6144]{1,0:T(8,128)(2,1)}, u32[]{:S(2)}) copy-start(bf16[48,6144]{1,0:T(8,128)(2,1)} %copy-done.1) | copy-start | bytes 1769476
Sparse Core Ops, SparseCore 0:
  11.8 53.9 all-gather.3
  67.4 49.9 all-gather.5
  142.7 194.0 all-reduce.2
  341.3 51.3 all-gather.7
where the time goes:
time: 430 us; the launch traced here: 429 us
  waiting for transfers between devices  308 us (72%)
  matrix products  72.1 us (17%)
  other arithmetic  16.9 us (4%)
  between operations  15.9 us (4%)
  local copies, waits for them, and re-layouts  10.1 us (2%)
  starting transfers between devices  5.99 us (1%)
    psum x1, waiting for transfers between devices, per_device(): lax.psum(jnp.dot(context, weight_out, preferred_element_type=jnp.float32)...  134 us
    ppermute x2, waiting for transfers between devices, partner(): return lax.ppermute(value, axis, pairs)  52.8 us
    all_gather x1, waiting for transfers between devices, per_device(): lax.all_gather(normed, 'tp', axis=0, tiled=True)  44.7 us
    all_gather x1, waiting for transfers between devices, per_device(): piece_cot = lax.all_gather(cotangents, 'tp', axis=0, tiled=True)  30.2 us
    ppermute x2, waiting for transfers between devices, passed_along(): lax.ppermute(array, axis, [(i, (i + by) % size) for i in range(size)])  24.6 us
    all_gather x1, waiting for transfers between devices, per_device(): piece_norm = lax.all_gather(stash_normed, 'tp', axis=0, tiled=True)  21.8 us
    dot_general x1, matrix products, per_device(): jnp.einsum('th,dh->td', value_back, weight_in, preferred_element_type=jnp...  14.5 us
    dot_general x1, matrix products, per_device(): jnp.einsum('td,th->dh', rows_norm, value_back, preferred_element_type=jnp...  9.91 us
  transfers between devices with their start and end apart: 8, of which 8 were waited for; matrix products, arithmetic and copies ran while one was open for 8% of the time, Pallas kernels for 0%

commit v1 on v0

--- a/solution.py
+++ b/solution.py
@@ -67,8 +67,12 @@
         preferred_element_type=jnp.float32,
     ).astype(jnp.bfloat16)
     context = mix_heads(causal_softmax(fwd_scores[0]), values)
-    summed = lax.psum(
-        jnp.dot(context, weight_out, preferred_element_type=jnp.float32).astype(jnp.bfloat16), "tp"
+    summed = jnp.sum(
+        lax.all_gather(
+            jnp.dot(context, weight_out, preferred_element_type=jnp.float32).astype(jnp.bfloat16),
+            "tp",
+        ),
+        axis=0,
     ).astype(jnp.float32)
     branch = lax.dynamic_slice_in_dim(summed, tp_index * share_rows, share_rows, 0)
     layer_out = (layer_rows + branch).astype(jnp.bfloat16)

time: 430 us -> 668 us (1.55)
  waiting for transfers between devices: 308 us -> 524 us
  other arithmetic: 16.9 us -> 32.5 us
    all_gather x0 -> x1, waiting for transfers between devices: none -> 304 us  [per_device(): lax.all_gather(jnp.dot(context, weight_out, preferred_element_type=jnp.fl...]
    psum x1, waiting for transfers between devices: 134 us -> 42.5 us  [per_device(): lax.psum(jnp.einsum('th,dh->td', value_back, weight_in, preferred_element...]
    all_gather x1, waiting for transfers between devices: 30.2 us -> 51.4 us  [per_device(): piece_cot = lax.all_gather(cotangents, 'tp', axis=0, tiled=True)]
    reduce_sum x0 -> x1, other arithmetic: none -> 15.8 us  [per_device(): jnp.sum(lax.all_gather(jnp.dot(context, weight_out, preferred_element_typ...]
    all_gather x1, waiting for transfers between devices: 21.8 us -> 11.8 us  [per_device(): piece_norm = lax.all_gather(stash_normed, 'tp', axis=0, tiled=True)]
    ppermute x2, waiting for transfers between devices: 24.6 us -> 17.7 us  [passed_along(): lax.ppermute(array, axis, [(i, (i + by) % size) for i in range(size)])]
  transfers between devices with their start and end apart: 8 -> 9, of which waited for: 8 -> 9; matrix products, arithmetic and copies ran while one was open for 8% -> 11% of each run, Pallas kernels for 0% -> 0%
where the time goes in v1:
time: 668 us
  waiting for transfers between devices  524 us (78%)
  matrix products  76.6 us (11%)
  other arithmetic  32.5 us (5%)
  between operations  15.9 us (2%)
  local copies, waits for them, and re-layouts  11.4 us (2%)
  starting transfers between devices  7.65 us (1%)
    all_gather x1, waiting for transfers between devices, per_device(): lax.all_gather(jnp.dot(context, weight_out, preferred_element_type=jnp.fl...  304 us
    ppermute x2, waiting for transfers between devices, partner(): return lax.ppermute(value, axis, pairs)  52.7 us
    all_gather x1, waiting for transfers between devices, per_device(): piece_cot = lax.all_gather(cotangents, 'tp', axis=0, tiled=True)  51.4 us
    all_gather x1, waiting for transfers between devices, per_device(): lax.all_gather(normed, 'tp', axis=0, tiled=True)  43.1 us
    psum x1, waiting for transfers between devices, per_device(): lax.psum(jnp.einsum('th,dh->td', value_back, weight_in, preferred_element...  42.5 us
    ppermute x2, waiting for transfers between devices, passed_along(): lax.ppermute(array, axis, [(i, (i + by) % size) for i in range(size)])  17.7 us
    reduce_sum x1, other arithmetic, per_device(): jnp.sum(lax.all_gather(jnp.dot(context, weight_out, preferred_element_typ...  15.8 us
    dot_general x1, matrix products, per_device(): jnp.einsum('th,dh->td', value_back, weight_in, preferred_element_type=jnp...  14.7 us
  transfers between devices with their start and end apart: 9, of which 9 were waited for; matrix products, arithmetic and copies ran while one was open for 11% of the time, Pallas kernels for 0%

profile of v1, /device:TPU:0, one launch (start us, length us, event | category | flops | bytes accessed | tf_op | source)
XLA Modules:
  0.0 667.8 jit_solution(3428280623607217348)
XLA Ops:
  7.2 3.0 copy.24
  10.3 2.1 fusion.65
  12.8 51.4 %all-gather.8.cloned.1.call-done = bf16[384,6144]{1,0:T(8,128)(2,1)} async-done(((bf16[48,6144]{1,0:T(8,128)(2,1)}), bf16[384,6144]{1,0:T(8,128)(2,1)}) %all-gather.8.cloned.1.call-update) | async-done | bytes 4718608 | tf_op jit(solution)/shard_map/all_gather | solution.py:93
  64.3 9.0 %fusion.44 = bf16[384,768]{1,0:T(8,128)(2,1)S(1)} fusion(bf16[384,6144]{1,0:T(8,128)(2,1)} %all-gather.8.cloned.1.call-done, bf16[1,768,6144]{2,1,0:T(8,128)(2,1)} %param.15), kind=kOutput, calls=%fused_computation.50 | convolution fusion | flops 3624173568 | bytes 14745600 | tf_op jit(solution)/shard_map/td,hd->th/dot_general | solution.py:100
  74.1 14.7 %fusion.14 = bf16[384,6144]{1,0:T(8,128)(2,1)} fusion(bf16[384,768]{0,1:T(8,128)(2,1)S(1)} %bitcast.104, bf16[1,6144,768]{2,1,0:T(8,128)(2,1)} %param.14), kind=kOutput, calls=%fused_computation.16 | convolution fusion | flops 3626237952 | bytes 14745600 | tf_op jit(solution)/shard_map/th,dh->td/dot_general | solution.py:121
  96.9 26.7 %collective-permute-done.1 = bf16[2,48,6144]{2,1,0:T(8,128)(2,1)} collective-permute-done((bf16[2,48,6144]{2,1,0:T(8,128)(2,1)S(1)}, bf16[2,48,6144]{2,1,0:T(8,128)(2,1)}, u32[]{:S(2)}, u32[]{:S(2)}) %collective-permute-start.1) | collective-permute-done | bytes 1179680 | tf_op jit(solution)/shard_map/ppermute | solution.py:18
  125.1 26.0 %collective-permute-done.2 = bf16[2,48,6144]{2,1,0:T(8,128)(2,1)S(1)} collective-permute-done((bf16[2,48,6144]{2,1,0:T(8,128)(2,1)}, bf16[2,48,6144]{2,1,0:T(8,128)(2,1)S(1)}, u32[]{:S(2)}, u32[]{:S(2)}) %collective-permute-start.2) | collective-permute-done | bytes 1179680 | tf_op jit(solution)/shard_map/ppermute | solution.py:18
  151.7 42.5 %all-reduce.2.cloned.1.call-done = bf16[384,6144]{1,0:T(8,128)(2,1)} async-done(((bf16[384,6144]{1,0:T(8,128)(2,1)}), bf16[384,6144]{1,0:T(8,128)(2,1)}) %all-reduce.2.cloned.1.call-update) | async-done | bytes 4718608 | tf_op jit(solution)/shard_map/psum | solution.py:120
  195.6 2.8 fusion.52
  198.7 5.9 fusion.64
  204.5 43.1 %all-gather.6.cloned.1.call-done = bf16[384,6144]{1,0:T(8,128)(2,1)} async-done(((bf16[48,6144]{1,0:T(8,128)(2,1)}), bf16[384,6144]{1,0:T(8,128)(2,1)}) %all-gather.6.cloned.1.call-update) | async-done | bytes 4718608 | tf_op jit(solution)/shard_map/all_gather | solution.py:65
  247.7 9.7 %fusion.38 = bf16[384,768]{1,0:T(8,128)(2,1)} fusion(bf16[384,6144]{1,0:T(8,128)(2,1)} %all-gather.6.cloned.1.call-done, bf16[1,6144,768]{2,1,0:T(8,128)(2,1)} %param.14), kind=kOutput, calls=%fused_computation.48 | convolution fusion | flops 3624173568 | bytes 14745600 | tf_op jit(solution)/shard_map/dot_general | solution.py:64
  257.4 2.1 copy.16
  259.5 2.9 fusion.37
  262.5 9.3 %fusion.17 = bf16[384,6144]{1,0:T(8,128)(2,1)} fusion(bf16[384,768]{0,1:T(8,128)(2,1)S(1)} %bitcast.102, bf16[1,768,6144]{2,1,0:T(8,128)(2,1)} %param.15), kind=kOutput, calls=%fused_computation.17 | convolution fusion | flops 3626237952 | bytes 14745600 | tf_op jit(solution)/shard_map/dot_general | solution.py:72
  271.8 2.7 collective-permute-start.3
  275.4 12.5 %collective-permute-done.3 = bf16[48,6144]{1,0:T(8,128)(2,1)} collective-permute-done((bf16[48,6144]{1,0:T(8,128)(2,1)}, bf16[48,6144]{1,0:T(8,128)(2,1)}, u32[]{:S(2)}, u32[]{:S(2)}) %collective-permute-start.3) | collective-permute-done | bytes 589856 | tf_op jit(solution)/shard_map/ppermute | solution.py:12
  287.9 11.8 %all-gather.10.cloned.1.call-done = bf16[384,6144]{1,0:T(8,128)(2,1)} async-done(((bf16[48,6144]{1,0:T(8,128)(2,1)}), bf16[384,6144]{1,0:T(8,128)(2,1)}) %all-gather.10.cloned.1.call-update) | async-done | bytes 4718608 | tf_op jit(solution)/shard_map/all_gather | solution.py:92
  299.7 8.9 %fusion.41 = bf16[384,768]{1,0:T(8,128)(2,1)S(1)} fusion(bf16[384,6144]{1,0:T(8,128)(2,1)} %all-gather.10.cloned.1.call-done, bf16[1,6144,768]{2,1,0:T(8,128)(2,1)} %param.14), kind=kOutput, calls=%fused_computation.49 | convolution fusion | flops 3624173568 | bytes 14745600 | tf_op jit(solution)/shard_map/dot_general | solution.py:96
  309.7 11.0 %fusion.12 = bf16[1,6144,768]{2,1,0:T(8,128)(2,1)} fusion(bf16[384,6144]{1,0:T(8,128)(2,1)} %all-gather.10.cloned.1.call-done, bf16[384,768]{0,1:T(8,128)(2,1)} %bitcast.105), kind=kOutput, calls=%fused_computation.14 | convolution fusion | flops 3628597248 | bytes 14745600 | tf_op jit(solution)/shard_map/td,th->dh/dot_general | solution.py:119
  320.7 304.4 %all-gather.12.cloned.1.call-done = bf16[3072,6144]{1,0:T(8,128)(2,1)} async-done(((bf16[384,6144]{1,0:T(8,128)(2,1)}), bf16[3072,6144]{1,0:T(8,128)(2,1)}) %all-gather.12.cloned.1.call-update) | async-done | bytes 37748752 | tf_op jit(solution)/shard_map/all_gather | solution.py:71
  625.1 15.8 %reduce_sum.96 = bf16[384,6144]{1,0:T(8,128)(2,1)} reduce(bf16[8,384,6144]{2,1,0:T(8,128)(2,1)} %bitcast.98, bf16[]{:T(256)} %constant.35.clone.1), dimensions={0}, to_apply=%region_4.5 | reduce | flops 16515072 | bytes 42467328 | tf_op jit(solution)/shard_map/reduce_sum | solution.py:70
  643.6 9.8 %fusion.13 = bf16[1,768,6144]{2,1,0:T(8,128)(2,1)} fusion(bf16[384,768]{0,1:T(8,128)(2,1)S(1)} %bitcast.106, bf16[384,6144]{1,0:T(8,128)(2,1)} %all-gather.8.cloned.1.call-done), kind=kOutput, calls=%fused_computation.15 | convolution fusion | flops 3628597248 | bytes 14745600 | tf_op jit(solution)/shard_map/th,td->hd/dot_general | solution.py:107
  653.4 5.2 collective-permute-done
  (47 shorter events, 18.5 us)
Async XLA Ops:
  7.2 3.1 copy-start.3
  7.2 57.1 %all-gather.8.cloned.1.call-start = ((), (), s32[]{:S(2)}) async-start(), calls=%async_computation.1 | async-start | bytes 5308416 | tf_op jit(solution)/shard_map/all_gather | solution.py:93
  10.2 183.9 %all-reduce.2.cloned.1.call-start = ((), (), s32[]{:S(2)}) async-start(), calls=%async_computation.2 | async-start | bytes 9437184 | tf_op jit(solution)/shard_map/psum | solution.py:120
  10.3 2.1 copy-start.2
  74.1 14.7 %copy-start.1 = (bf16[6,128,384]{2,1,0:T(8,128)(2,1)}, bf16[6,128,384]{2,1,0:T(8,128)(2,1)S(1)}, u32[]{:S(2)}) copy-start(bf16[6,128,384]{2,1,0:T(8,128)(2,1)S(1)} %convolution_convert_fusion.3) | copy-start | bytes 1769476
  88.8 1.1 copy-start
  88.8 2.7 copy-start.4
  88.9 158.8 %all-gather.6.cloned.1.call-start = ((), (), s32[]{:S(2)}) async-start(), calls=%async_computation | async-start | bytes 5308416 | tf_op jit(solution)/shard_map/all_gather | solution.py:65
  91.5 208.2 %all-gather.10.cloned.1.call-start = ((), (), s32[]{:S(2)}) async-start(), calls=%async_computation.3 | async-start | bytes 5308416 | tf_op jit(solution)/shard_map/all_gather | solution.py:92
  95.4 28.3 %collective-permute-start.1 = (bf16[2,48,6144]{2,1,0:T(8,128)(2,1)S(1)}, bf16[2,48,6144]{2,1,0:T(8,128)(2,1)}, u32[]{:S(2)}, u32[]{:S(2)}) collective-permute-start(bf16[2,48,6144]{2,1,0:T(8,128)(2,1)S(1)} %pad_maximum_fusion), channel_id=1, source_target_pairs={{0,8},{8,0},{16,24},{24,16},{1,9},{9,1},{17,25},{25,17},{2,10},{10... | collective-permute-start | bytes 3538952 | tf_op jit(solution)/shard_map/ppermute | solution.py:18
  123.7 27.5 %collective-permute-start.2 = (bf16[2,48,6144]{2,1,0:T(8,128)(2,1)}, bf16[2,48,6144]{2,1,0:T(8,128)(2,1)S(1)}, u32[]{:S(2)}, u32[]{:S(2)}) collective-permute-start(bf16[2,48,6144]{2,1,0:T(8,128)(2,1)} %collective-permute-done.1), channel_id=1, source_target_pairs={{0,16},{8,24},{16,0},{24,8},{1,17},{9,25},{17,1},{25,9},{2,18},{10... | collective-permute-start | bytes 3538952 | tf_op jit(solution)/shard_map/ppermute | solution.py:18
  198.4 426.7 %all-gather.12.cloned.1.call-start = ((), (), s32[]{:S(2)}) async-start(), calls=%async_computation.4 | async-start | bytes 42467328 | tf_op jit(solution)/shard_map/all_gather | solution.py:71
  271.8 16.1 %collective-permute-start.3 = (bf16[48,6144]{1,0:T(8,128)(2,1)}, bf16[48,6144]{1,0:T(8,128)(2,1)}, u32[]{:S(2)}, u32[]{:S(2)}) collective-permute-start(bf16[48,6144]{1,0:T(8,128)(2,1)} %get-tuple-element.8), channel_id=1, source_target_pairs={{0,24},{8,0},{16,8},{24,16},{1,25},{9,1},{17,9},{25,17},{2,26},{10... | collective-permute-start | bytes 1769480 | tf_op jit(solution)/shard_map/ppermute | solution.py:12
  642.1 16.4 %collective-permute-start = (bf16[48,6144]{1,0:T(8,128)(2,1)S(1)}, bf16[48,6144]{1,0:T(8,128)(2,1)S(1)}, u32[]{:S(2)}, u32[]{:S(2)}) collective-permute-start(bf16[48,6144]{1,0:T(8,128)(2,1)S(1)} %fusion.59), channel_id=1, source_target_pairs={{0,8},{8,16},{16,24},{24,0},{1,9},{9,17},{17,25},{25,1},{2,10},{10... | collective-permute-start | bytes 1769480 | tf_op jit(solution)/shard_map/ppermute | solution.py:12
Sparse Core Ops, SparseCore 0:
  10.3 53.9 all-gather.7
  89.0 105.1 all-reduce.1
  196.4 51.2 all-gather.5
  249.7 49.9 all-gather.9
  301.8 323.2 all-gather.11
